TPU v7x, 256 devices: a whole 4x4x8 slice. The times are simulated.
256 devices in a mesh: ctx: 64 (over y, x, z_hi), ch: 2 (over core), fsdp: 2 (over z_lo).
Axes of the slice: x: 4, y: 4, z: 8 (z_hi: 4, z_lo: 2; z = z_hi * 2 + z_lo), core: 2. Of those that a mesh axis runs over, the one named last changes fastest.
Arguments:
- query_rows: bfloat16 [16384, 8192], P(('ctx', 'fsdp'), 'ch'), may hold values from -6 to 6
- key_rows: bfloat16 [16384, 8192], P(('ctx', 'fsdp'), 'ch'), may hold values from -6 to 6
- value_rows: bfloat16 [16384, 8192], P(('ctx', 'fsdp'), 'ch'), may hold values from -6 to 6
- upstream: bfloat16 [16384, 8192], P(('ctx', 'fsdp'), 'ch'), may hold values from -6 to 6
- decay_rate: float32 [8, 512], P(None, 'fsdp'), may hold values from 0.1 to 341
- residue: float32 [8, 512], P(None, 'fsdp'), may hold values from -4 to 4
Outputs:
- grad_query: bfloat16 [16384, 8192], P(('ctx', 'fsdp'), 'ch')
- grad_key: bfloat16 [16384, 8192], P(('ctx', 'fsdp'), 'ch')
- grad_value: bfloat16 [16384, 8192], P(('ctx', 'fsdp'), 'ch')
- residue_grad: float32 [8, 512], P(None, 'fsdp')
All inputs are finite; a program needn't handle non-finite values.
Results may differ from a plain program's by a relative error of at most 0.0017.
Values sent between devices are 32-bit elements; how exact they have to be, the bound alone decides.
No kernel may reach another device: no remote copies, remote signals or barrier semaphores. Data moves between devices by JAX's collectives and lax.ppermute only.
A program may use at most 128 MiB of HBM per device.

v0:
```python
import math
import jax
import jax.numpy as jnp
from jax import lax
from jax.sharding import PartitionSpec as P


def carried_in(part, axis, combine, identity, reverse):
    count = lax.axis_size(axis)
    place = lax.axis_index(axis)
    ahead = count - 1 - place if reverse else place
    gathered = jax.tree.map(lambda a: lax.all_gather(a, axis), part)
    state = jax.tree.map(lambda a, e: jnp.zeros_like(a) + jnp.asarray(e, a.dtype), part, identity)

    def one(lap, state):
        source = count - 1 - lap if reverse else lap
        return combine(
            state, jax.tree.map(lambda a: lax.dynamic_index_in_dim(a, source, 0, False), gathered)
        )

    return lax.fori_loop(0, ahead, one, state)


def to_blocks(matrix, block_count, width):
    return matrix.reshape(matrix.shape[0], block_count, width).transpose(1, 0, 2)


def from_blocks(blocked):
    return blocked.transpose(1, 0, 2).reshape(blocked.shape[1], -1)


def local(query_rows, key_rows, value_rows, upstream, decay_rate, residue):
    rates, residues = (
        lax.all_gather(decay_rate, "fsdp", axis=1, tiled=True),
        lax.all_gather(residue, "fsdp", axis=1, tiled=True),
    )
    row_count = query_rows.shape[0]
    local_width = query_rows.shape[1]
    width = rates.shape[1]
    modes = rates.shape[0]
    block_count = local_width // width
    tokens = row_count * lax.axis_size("ctx") * lax.axis_size("fsdp")
    log_decay = rates / tokens
    mode_gain = jnp.sqrt((1.0 + rates) / tokens)
    weight = residues * mode_gain
    positions = jnp.arange(row_count, dtype=jnp.float32)[:, None, None]
    blocks = tuple(
        (
            to_blocks(matrix, block_count, width)
            for matrix in (query_rows, key_rows, value_rows, upstream)
        )
    )
    span = min(row_count, 128)
    steps_in = jnp.arange(span, dtype=jnp.float32)[:, None, None]
    rising = jnp.exp(log_decay * steps_in)
    falling = jnp.exp(-log_decay * steps_in)
    index_row = jnp.arange(span)[:, None]
    index_col = jnp.arange(span)[None, :]
    lower_ones = (index_row >= index_col).astype(jnp.float32)
    upper_ones = (index_row <= index_col).astype(jnp.float32)
    enter_next = jnp.exp(-log_decay * (steps_in + 1.0))
    enter_prior = jnp.exp(-log_decay * (span - steps_in))

    def summarize(block):
        query_part, key_part, value_part, grad_part = block
        product = key_part.astype(jnp.float32) * value_part.astype(jnp.float32)
        gated = grad_part.astype(jnp.float32) * query_part.astype(jnp.float32)
        tail = jnp.exp(-log_decay * (row_count - 1.0 - positions))
        head = jnp.exp(-log_decay * positions)
        return (
            jnp.sum(tail * product[:, None, :], axis=0),
            jnp.sum(head * gated[:, None, :], axis=0),
        )

    ahead, behind = lax.map(summarize, blocks)

    def combine(earlier, later):
        return (earlier[0] + later[0], later[1] + jnp.exp(-log_decay * later[0][0]) * earlier[1])

    identity = (jnp.zeros((1,), jnp.float32), jnp.zeros_like(ahead))
    single = jnp.full((1,), float(row_count), jnp.float32)
    carry_ahead = carried_in((single, ahead), ("ctx", "fsdp"), combine, identity, False)[1]
    carry_behind = carried_in((single, behind), ("ctx", "fsdp"), combine, identity, True)[1]

    def running(ones, scaled):
        flat = scaled.reshape(span, -1)
        summed = jnp.dot(
            ones, flat, precision=lax.Precision.HIGHEST, preferred_element_type=jnp.float32
        )
        return summed.reshape(span, modes, width)

    def finish(block):
        query_part, key_part, value_part, grad_part, enter_ahead, enter_behind = block
        product = key_part.astype(jnp.float32) * value_part.astype(jnp.float32)
        gated = grad_part.astype(jnp.float32) * query_part.astype(jnp.float32)
        state = enter_ahead
        terms = jnp.zeros((modes, width), jnp.float32)
        states = falling * running(lower_ones, rising * product[:, None, :]) + enter_next * state
        conv_parts = [jnp.sum(weight * states, axis=1)]
        terms = terms + jnp.sum(gated[:, None, :] * states, axis=0)
        state = enter_behind
        flow_parts = []
        states = rising * running(upper_ones, falling * gated[:, None, :]) + enter_prior * state
        flow_parts.insert(0, jnp.sum(weight * states, axis=1))
        conv = jnp.concatenate(conv_parts, axis=0)
        flowing = jnp.concatenate(flow_parts, axis=0)
        grad_q = (grad_part.astype(jnp.float32) * conv).astype(jnp.bfloat16)
        grad_k = (flowing * value_part.astype(jnp.float32)).astype(jnp.bfloat16)
        grad_v = (flowing * key_part.astype(jnp.float32)).astype(jnp.bfloat16)
        return (grad_q, grad_k, grad_v, terms)

    query_grads, key_grads, value_grads, all_terms = lax.map(
        finish, blocks + (carry_ahead, carry_behind)
    )
    partial_grad = mode_gain * jnp.sum(all_terms, axis=0) / math.sqrt(tokens)
    summed = lax.psum(partial_grad, ("ctx", "ch"))
    residue_grad = lax.psum_scatter(summed, "fsdp", scatter_dimension=1, tiled=True)
    return (
        from_blocks(query_grads),
        from_blocks(key_grads),
        from_blocks(value_grads),
        residue_grad,
    )


def solution(mesh):
    placed = (
        P(("ctx", "fsdp"), "ch"),
        P(("ctx", "fsdp"), "ch"),
        P(("ctx", "fsdp"), "ch"),
        P(("ctx", "fsdp"), "ch"),
        P(None, "fsdp"),
        P(None, "fsdp"),
    )
    return jax.shard_map(
        local,
        mesh=mesh,
        in_specs=placed,
        out_specs=(
            P(("ctx", "fsdp"), "ch"),
            P(("ctx", "fsdp"), "ch"),
            P(("ctx", "fsdp"), "ch"),
            P(None, "fsdp"),
        ),
        check_vma=False,
    )
```

profile of v0, /device:TPU:32, one launch (start us, length us, event | category | flops | bytes accessed | tf_op | source)
XLA Modules:
  0.0 1259.8 jit_solution(2737631735284426398)
XLA Ops:
  7.2 4.7 all_gather.23
  11.9 4.6 all_gather.22
  16.5 1.7 copy.34
  20.2 1.6 copy.33
  23.8 36.9 %while.64 = (s32[]{:T(128)}, f32[8,8,512]{2,1,0:T(8,128)}, f32[8,8,512]{2,1,0:T(8,128)}, f32[1,8,512]{2,1,0:T(8,128)}, bf16[8,128,512]{1,2,0:T(8,128)(2,1)S(1)},...) while((s32[]{:T(128)}, f32[8,8,512]{2,1,0:T(8,128)}, ...), condition=%wide.region_3.4_spmd.clone.clone, body=%wide.region_0.3_spmd.clone.clone.sunk | while | flops 3530882 | bytes 3786349 | solution.py:75
  26.0 1.7 fusion.52
  30.7 1.7 fusion.52
  35.3 1.7 fusion.52
  39.9 1.7 fusion.52
  44.5 1.7 fusion.52
  49.1 1.7 fusion.52
  53.7 1.7 fusion.52
  58.3 1.7 fusion.52
  63.5 350.4 %all-reduce = f32[128]{0:T(128)S(1)} all-reduce(f32[128]{0:T(128)S(1)} %dynamic-update-slice), channel_id=1, replica_groups=mesh['ctx'=64,'ch'=2,'fsdp'=2] {'ctx','fsdp'}, use_global_device_ids=true, to_apply=%add | all-reduce | flops 128 | bytes 1024
  414.0 372.6 %while.63 = (s32[]{:T(128)}, f32[8,8,512]{2,1,0:T(8,128)S(1)}, s32[]{:T(128)}, f32[128,8,8,512]{3,2,1,0:T(8,128)}, f32[128,1]{0,1:T(1,128)S(1)}, /*index=5*/f32[...) while((s32[]{:T(128)}, f32[8,8,512]{2,1,0:T(8,128)S(1)}, s32[]{:T(128)}, ...), condition=%wide.region_7.8_spmd, body=%wide.region_6.7_spmd.sunk | while | flops 69638 | bytes 442535 | solution.py:21
  414.6 1.4 exponential_bitcast_fusion.5
  417.6 1.4 exponential_bitcast_fusion.5
  420.5 1.4 exponential_bitcast_fusion.5
  423.5 1.4 exponential_bitcast_fusion.5
  426.4 1.4 exponential_bitcast_fusion.5
  429.4 1.4 exponential_bitcast_fusion.5
  432.3 1.4 exponential_bitcast_fusion.5
  435.3 1.4 exponential_bitcast_fusion.5
  438.3 1.4 exponential_bitcast_fusion.5
  441.2 1.4 exponential_bitcast_fusion.5
  444.2 1.4 exponential_bitcast_fusion.5
  447.1 1.4 exponential_bitcast_fusion.5
  450.1 1.4 exponential_bitcast_fusion.5
  453.0 1.4 exponential_bitcast_fusion.5
  479.7 1.4 exponential_bitcast_fusion.5
  535.8 1.4 exponential_bitcast_fusion.5
  592.0 1.4 exponential_bitcast_fusion.5
  648.2 1.4 exponential_bitcast_fusion.5
  704.4 1.4 exponential_bitcast_fusion.5
  760.6 1.4 exponential_bitcast_fusion.5
  786.6 2.9 while.62
  790.2 94.5 %while.65 = (s32[]{:T(128)}, bf16[8,128,512]{1,2,0:T(8,128)(2,1)}, bf16[8,128,512]{1,2,0:T(8,128)(2,1)}, bf16[8,128,512]{1,2,0:T(8,128)(2,1)}, f32[8,8,512]{2,1,...) while((s32[]{:T(128)}, bf16[8,128,512]{1,2,0:T(8,128)(2,1)}, ...), condition=%wide.region_12.13_spmd.clone.clone, body=%wide.region_8.12_spmd.clone.clone.sunk | while | flops 1624109056 | bytes 28904616 | solution.py:112
  792.4 2.3 fusion.58
  794.7 1.8 fusion.59
  796.5 3.4 fusion.60
  804.3 2.3 fusion.58
  806.5 1.8 fusion.59
  808.4 3.4 fusion.60
  816.1 2.3 fusion.58
  818.3 1.8 fusion.59
  820.2 3.4 fusion.60
  827.9 2.3 fusion.58
  830.1 1.8 fusion.59
  832.0 3.4 fusion.60
  839.7 2.3 fusion.58
  842.0 1.8 fusion.59
  843.8 3.4 fusion.60
  851.5 2.2 fusion.58
  853.7 1.8 fusion.59
  855.6 3.4 fusion.60
  863.3 2.3 fusion.58
  865.6 1.8 fusion.59
  867.4 3.4 fusion.60
  875.1 2.3 fusion.58
  877.4 1.8 fusion.59
  879.2 3.4 fusion.60
  886.4 2.4 copy.43
  891.3 6.6 reduce-scatter.2.cloned.1.call-done
  898.0 355.3 %psum.8 = f32[8,256]{1,0:T(8,128)} all-reduce(f32[8,256]{1,0:T(8,128)} %reduce-scatter.2.cloned.1.call-done), channel_id=1, replica_groups=mesh['ctx'=64,'ch'=2,'fsdp'=2] {'ctx','ch'}, use_global_device_ids=true, to_apply=%region_14.15 | all-reduce | flops 2048 | bytes 16384 | tf_op jit(solution)/shard_map/psum | solution.py:116
  (580 shorter events, 413.0 us)
Async XLA Ops:
  7.2 11.0 copy-start.1
  7.2 406.7 %all-gather.7.cloned.1.call-start = ((), (), s32[]{:S(2)}) async-start(), calls=%async_computation.2 | async-start | bytes 16908288 | tf_op jit(solution)/shard_map/all_gather | solution.py:12
  11.9 9.9 copy-start.6
  16.5 3.0 copy-start.2
  60.7 725.8 %all-gather.5.cloned.1.call-start = ((), (), s32[]{:S(2)}) async-start(), calls=%async_computation.1 | async-start | bytes 16908288 | tf_op jit(solution)/shard_map/all_gather | solution.py:12
  61.5 836.5 %reduce-scatter.2.cloned.1.call-start = ((), (), s32[]{:S(2)}) async-start(), calls=%async_computation.3 | async-start | bytes 24576 | tf_op jit(solution)/shard_map/reduce_scatter | solution.py:117
  413.9 376.2 %copy-start = (f32[8,512]{1,0:T(8,128)S(1)}, f32[8,512]{1,0:T(8,128)}, u32[]{:S(2)}) copy-start(f32[8,512]{1,0:T(8,128)} %get-tuple-element.1009) | copy-start | bytes 49156
  414.0 376.2 %copy-start.5 = (f32[8,512]{1,0:T(8,128)S(1)}, f32[8,512]{1,0:T(8,128)}, u32[]{:S(2)}) copy-start(f32[8,512]{1,0:T(8,128)} %get-tuple-element.1003) | copy-start | bytes 49156
  790.2 95.5 %copy-start.7 = (f32[8,512]{1,0:T(8,128)S(1)}, f32[8,512]{1,0:T(8,128)}, u32[]{:S(2)}) copy-start(f32[8,512]{1,0:T(8,128)} %copy-done.6) | copy-start | bytes 49156
  884.7 4.0 copy-start.3
  886.4 3.7 copy-start.4
Sparse Core Ops, SparseCore 0:
  60.8 151.9 all-gather.6
  216.5 147.9 all-gather.4
  886.5 11.4 reduce-scatter.1
where the time goes:
time: 1270 us; the launch traced here: 1260 us
  blocking collectives  715 us (56%)
  other arithmetic  373 us (29%)
  local copies, waits for them, and re-layouts  113 us (9%)
  matrix products  32.6 us (3%)
  between operations  13.9 us (1%)
    psum x1, blocking collectives, local(): summed = lax.psum(partial_grad, ('ctx', 'ch'))  355 us
    unnamed x1, blocking collectives  350 us
    exp x127, other arithmetic, combine(): jnp.exp(-log_decay * later[0][0]) * earlier[1]  172 us
    add x127, other arithmetic, combine(): later[1] + jnp.exp(-log_decay * later[0][0]) * earlier[1]  122 us
    dynamic_slice x127, local copies, waits for them, and re-layouts, one(): lax.dynamic_index_in_dim(a, source, 0, False)  77.7 us
    dot_general x16, matrix products, running(): jnp.dot(ones, flat, precision=lax.Precision.HIGHEST, preferred_element_ty...  32.6 us
    reduce_sum x8, other arithmetic, finish(): flow_parts.insert(0, jnp.sum(weight * states, axis=1))  27.3 us
  transfers between devices with their start and end apart: 3, of which 1 were waited for; matrix products, arithmetic and copies ran while one was open for 30% of the time, Pallas kernels for 0%

commit v1 on v0

--- a/solution.py
+++ b/solution.py
@@ -3,6 +3,7 @@
 import jax.numpy as jnp
 from jax import lax
 from jax.sharding import PartitionSpec as P
+from jax.lax import psum
 
 
 def carried_in(part, axis, combine, identity, reverse):
@@ -113,7 +114,7 @@
         finish, blocks + (carry_ahead, carry_behind)
     )
     partial_grad = mode_gain * jnp.sum(all_terms, axis=0) / math.sqrt(tokens)
-    summed = lax.psum(partial_grad, ("ctx", "ch"))
+    summed = psum(psum(partial_grad, "ch"), "ctx")
     residue_grad = lax.psum_scatter(summed, "fsdp", scatter_dimension=1, tiled=True)
     return (
         from_blocks(query_grads),

time: 1270 us -> 1120 us (0.88)
  blocking collectives: 715 us -> 559 us
    psum x1 -> x2, blocking collectives: 355 us -> 199 us  [local(): summed = psum(psum(partial_grad, 'ch'), 'ctx')]
  transfers between devices with their start and end apart: 3 -> 3, of which waited for: 1 -> 1; matrix products, arithmetic and copies ran while one was open for 30% -> 34% of each run, Pallas kernels for 0% -> 0%
where the time goes in v1:
time: 1120 us; the launch traced here: 1100 us
  blocking collectives  559 us (50%)
  other arithmetic  370 us (33%)
  local copies, waits for them, and re-layouts  114 us (10%)
  matrix products  32.5 us (3%)
  between operations  13.9 us (1%)
    unnamed x1, blocking collectives  350 us
    psum x2, blocking collectives, local(): summed = psum(psum(partial_grad, 'ch'), 'ctx')  199 us
    exp x127, other arithmetic, combine(): jnp.exp(-log_decay * later[0][0]) * earlier[1]  169 us
    add x127, other arithmetic, combine(): later[1] + jnp.exp(-log_decay * later[0][0]) * earlier[1]  122 us
    dynamic_slice x127, local copies, waits for them, and re-layouts, one(): lax.dynamic_index_in_dim(a, source, 0, False)  78.3 us
    dot_general x16, matrix products, running(): jnp.dot(ones, flat, precision=lax.Precision.HIGHEST, preferred_element_ty...  32.5 us
    reduce_sum x8, other arithmetic, finish(): flow_parts.insert(0, jnp.sum(weight * states, axis=1))  27.3 us
  transfers between devices with their start and end apart: 3, of which 1 were waited for; matrix products, arithmetic and copies ran while one was open for 34% of the time, Pallas kernels for 0%

profile of v1, /device:TPU:32, one launch (start us, length us, event | category | flops | bytes accessed | tf_op | source)
XLA Modules:
  0.0 1103.2 jit_solution(15633426720602658693)
XLA Ops:
  7.2 4.7 all_gather.23
  11.9 4.6 all_gather.22
  16.5 1.7 copy.34
  20.2 1.6 copy.33
  23.8 36.9 %while.64 = (s32[]{:T(128)}, f32[8,8,512]{2,1,0:T(8,128)}, f32[8,8,512]{2,1,0:T(8,128)}, f32[1,8,512]{2,1,0:T(8,128)}, bf16[8,128,512]{1,2,0:T(8,128)(2,1)S(1)},...) while((s32[]{:T(128)}, f32[8,8,512]{2,1,0:T(8,128)}, ...), condition=%wide.region_3.4_spmd.clone.clone, body=%wide.region_0.3_spmd.clone.clone.sunk | while | flops 3530882 | bytes 3786349 | solution.py:76
  26.0 1.7 fusion.52
  30.6 1.7 fusion.52
  35.2 1.7 fusion.52
  39.8 1.7 fusion.52
  44.5 1.7 fusion.52
  49.1 1.7 fusion.52
  53.7 1.7 fusion.52
  58.3 1.7 fusion.52
  63.6 350.3 %all-reduce = f32[128]{0:T(128)S(1)} all-reduce(f32[128]{0:T(128)S(1)} %dynamic-update-slice), channel_id=1, replica_groups=mesh['ctx'=64,'ch'=2,'fsdp'=2] {'ctx','fsdp'}, use_global_device_ids=true, to_apply=%add | all-reduce | flops 128 | bytes 1024
  414.0 369.8 %while.63 = (s32[]{:T(128)}, f32[8,8,512]{2,1,0:T(8,128)S(1)}, s32[]{:T(128)}, f32[128,8,8,512]{3,2,1,0:T(8,128)}, f32[128,1]{0,1:T(1,128)S(1)}, /*index=5*/f32[...) while((s32[]{:T(128)}, f32[8,8,512]{2,1,0:T(8,128)S(1)}, s32[]{:T(128)}, ...), condition=%wide.region_7.8_spmd, body=%wide.region_6.7_spmd.sunk | while | flops 69638 | bytes 442535 | solution.py:22
  414.6 1.3 exponential_bitcast_fusion.5
  417.5 1.3 exponential_bitcast_fusion.5
  435.1 1.3 exponential_bitcast_fusion.5
  452.8 1.3 exponential_bitcast_fusion.5
  455.7 1.3 exponential_bitcast_fusion.5
  470.4 1.3 exponential_bitcast_fusion.5
  473.3 1.3 exponential_bitcast_fusion.5
  490.9 1.3 exponential_bitcast_fusion.5
  508.5 1.3 exponential_bitcast_fusion.5
  511.5 1.3 exponential_bitcast_fusion.5
  526.1 1.3 exponential_bitcast_fusion.5
  529.1 1.3 exponential_bitcast_fusion.5
  546.7 1.3 exponential_bitcast_fusion.5
  564.3 1.3 exponential_bitcast_fusion.5
  567.2 1.3 exponential_bitcast_fusion.5
  581.9 1.3 exponential_bitcast_fusion.5
  584.8 1.3 exponential_bitcast_fusion.5
  602.5 1.3 exponential_bitcast_fusion.5
  783.9 3.0 while.62
  784.5 1.4 exponential_bitcast_fusion.4
  787.5 94.5 %while.65 = (s32[]{:T(128)}, bf16[8,128,512]{1,2,0:T(8,128)(2,1)}, bf16[8,128,512]{1,2,0:T(8,128)(2,1)}, bf16[8,128,512]{1,2,0:T(8,128)(2,1)}, f32[8,8,512]{2,1,...) while((s32[]{:T(128)}, bf16[8,128,512]{1,2,0:T(8,128)(2,1)}, ...), condition=%wide.region_12.13_spmd.clone.clone, body=%wide.region_8.12_spmd.clone.clone.sunk | while | flops 1624109056 | bytes 28904616 | solution.py:113
  789.7 2.3 fusion.58
  792.0 1.8 fusion.59
  793.8 3.4 fusion.60
  801.5 2.3 fusion.58
  803.8 1.8 fusion.59
  805.6 3.4 fusion.60
  813.3 2.3 fusion.58
  815.6 1.8 fusion.59
  817.4 3.4 fusion.60
  825.1 2.3 fusion.58
  827.4 1.8 fusion.59
  829.2 3.4 fusion.60
  837.0 2.3 fusion.58
  839.2 1.8 fusion.59
  841.1 3.4 fusion.60
  848.8 2.3 fusion.58
  851.0 1.8 fusion.59
  852.9 3.4 fusion.60
  860.6 2.2 fusion.58
  862.8 1.8 fusion.59
  864.7 3.4 fusion.60
  872.4 2.2 fusion.58
  874.6 1.8 fusion.59
  876.5 3.4 fusion.60
  883.6 2.4 copy.43
  888.6 8.6 reduce-scatter.2.cloned.1.call-done
  897.2 2.6 psum.17
  899.8 196.9 %psum.16 = f32[8,256]{1,0:T(8,128)} all-reduce(f32[8,256]{1,0:T(8,128)S(1)} %psum.17), channel_id=1, replica_groups=mesh['ctx'=64,'ch'=2,'fsdp'=2] {'ctx'}, use_global_device_ids=true, to_apply=%region_15.16 | all-reduce | flops 2048 | bytes 16384 | tf_op jit(solution)/shard_map/psum | solution.py:117
  (581 shorter events, 412.2 us)
Async XLA Ops:
  7.2 11.0 %copy-start.1 = (bf16[128,4096]{1,0:T(8,128)(2,1)S(1)}, bf16[128,4096]{1,0:T(8,128)(2,1)}, u32[]{:S(2)}) copy-start(bf16[128,4096]{1,0:T(8,128)(2,1)} %param.14) | copy-start | bytes 3145732
  7.2 406.7 %all-gather.7.cloned.1.call-start = ((), (), s32[]{:S(2)}) async-start(), calls=%async_computation.2 | async-start | bytes 16908288 | tf_op jit(solution)/shard_map/all_gather | solution.py:13
  11.9 9.9 copy-start.6
  16.5 3.0 copy-start.2
  60.7 723.2 %all-gather.5.cloned.1.call-start = ((), (), s32[]{:S(2)}) async-start(), calls=%async_computation.1 | async-start | bytes 16908288 | tf_op jit(solution)/shard_map/all_gather | solution.py:13
  61.4 835.8 %reduce-scatter.2.cloned.1.call-start = ((), (), s32[]{:S(2)}) async-start(), calls=%async_computation.3 | async-start | bytes 24576 | tf_op jit(solution)/shard_map/reduce_scatter | solution.py:118
  413.9 373.5 %copy-start = (f32[8,512]{1,0:T(8,128)S(1)}, f32[8,512]{1,0:T(8,128)}, u32[]{:S(2)}) copy-start(f32[8,512]{1,0:T(8,128)} %get-tuple-element.1009) | copy-start | bytes 49156
  413.9 373.5 %copy-start.5 = (f32[8,512]{1,0:T(8,128)S(1)}, f32[8,512]{1,0:T(8,128)}, u32[]{:S(2)}) copy-start(f32[8,512]{1,0:T(8,128)} %get-tuple-element.1003) | copy-start | bytes 49156
  787.5 95.5 %copy-start.7 = (f32[8,512]{1,0:T(8,128)S(1)}, f32[8,512]{1,0:T(8,128)}, u32[]{:S(2)}) copy-start(f32[8,512]{1,0:T(8,128)} %copy-done.6) | copy-start | bytes 49156
  882.0 4.0 copy-start.3
  883.6 3.7 copy-start.4
Sparse Core Ops, SparseCore 0:
  60.8 151.7 all-gather.6
  216.3 147.9 all-gather.4
  883.7 13.4 reduce-scatter.1
